TPU v7x, 32 devices: a whole 2x2x4 slice. The times are simulated.
32 devices in a mesh: groups: 2 (over y), shot: 4 (over x, core), slab: 4 (over z).
Axes of the slice: x: 2, y: 2, z: 4, core: 2. Of those that a mesh axis runs over, the one named last changes fastest.
Arguments:
- slowness: float32 [32, 192, 128], P(('groups', 'slab')), parts along dimension 0, may hold values from 0.8 to 1.25
- wave_prev: float32 [8, 16, 192, 128], P(('groups', 'shot'), 'slab'), parts along dimension 0, may hold values from -6 to 6
- wave_now: float32 [8, 16, 192, 128], P(('groups', 'shot'), 'slab'), parts along dimension 0, may hold values from -6 to 6
- memory: float32 [8, 3, 16, 192, 128], P(('groups', 'shot'), None, 'slab'), parts along dimension 0, may hold values from -6 to 6
- adjoint_now: float32 [8, 16, 192, 128], P(('groups', 'shot'), 'slab'), parts along dimension 0, may hold values from -6 to 6
- adjoint_prev: float32 [8, 16, 192, 128], P(('groups', 'shot'), 'slab'), parts along dimension 0, may hold values from -6 to 6
- wavelet: float32 [4], replicated, may hold values from -16 to 16
- src_cells: int32 [8, 64], P(('groups', 'shot')), parts along dimension 0, may hold values from 0 to 393215
- src_signs: int32 [8, 64], P(('groups', 'shot')), parts along dimension 0, may hold values from -1 to 1, as said below
- rec_cells: int32 [512], P('groups'), parts along dimension 0, may hold values from 0 to 393215
- observed: float32 [8, 4, 256], P(('groups', 'shot')), parts along dimension 0, may hold values from -6 to 6
Outputs:
- new_slowness: float32 [32, 192, 128], P(('groups', 'slab')), parts along dimension 0
- gradient: float32 [32, 192, 128], P(('groups', 'slab'), 'shot'), parts along dimension 0
There are 2 independent parts, one for each index of `groups`. A program takes and returns all parts, laid end to end along the dimension named above; an argument that names none is the same for every part. Nothing has to cross between parts.
Inputs may be any that keep to these rules, and one draw needn't show every extreme that they name: `src_signs`: each entry is -1 or +1.
All inputs are finite; a program needn't handle non-finite values.
Results may differ from a plain program's by a relative error of at most 0.0001.
Values sent between devices are 32-bit elements; how exact they have to be, the bound alone decides.
No kernel may reach another device: no remote copies, remote signals or barrier semaphores. Data moves between devices by JAX's collectives and lax.ppermute only.
A program may use at most 64 MiB of HBM per device.

v0:
```python
import jax
import jax.numpy as jnp
from jax import lax
from jax.sharding import PartitionSpec as P

STEPS = 4
center_coef = -2.5
near_coef = 4.0 / 3.0
far_coef = -1.0 / 12.0
courant = 0.14
relax_decay = (0.3, 0.7, 0.95)
relax_weight = (0.3, 0.2, 0.1)
update_rate = 0.05
tiny_eps = 1e-06


def padded_2(block, sides, width):
    for axis, dim in sides:
        count = lax.axis_size(axis)
        forward = [(i, i + 1) for i in range(count - 1)]
        backward = [(target, source) for source, target in forward]
        low = lax.ppermute(
            lax.slice_in_dim(block, block.shape[dim] - width, None, axis=dim), axis, forward
        )
        high = lax.ppermute(lax.slice_in_dim(block, 0, width, axis=dim), axis, backward)
        block = jnp.concatenate([low, block, high], axis=dim)
    return block


def laplace(padded):
    middle = padded[2:-2]
    flanks = jnp.pad(middle, ((0, 0), (2, 2), (2, 2)))
    depth_sum = near_coef * (padded[3:-1] + padded[1:-3]) + far_coef * (padded[4:] + padded[:-4])
    cross_sum = near_coef * (flanks[:, 3:-1, 2:-2] + flanks[:, 1:-3, 2:-2]) + far_coef * (
        flanks[:, 4:, 2:-2] + flanks[:, :-4, 2:-2]
    )
    along_sum = near_coef * (flanks[:, 2:-2, 3:-1] + flanks[:, 2:-2, 1:-3]) + far_coef * (
        flanks[:, 2:-2, 4:] + flanks[:, 2:-2, :-4]
    )
    return 3.0 * center_coef * middle + depth_sum + cross_sum + along_sum


def place_sources(cells, signs, start, count):
    local = cells - start
    inside = (local >= 0) & (local < count)
    slot = jnp.where(inside, local, count)
    return jnp.zeros((count,), jnp.float32).at[slot].add(signs.astype(jnp.float32), mode="drop")


def per_device(
    slowness,
    wave_prev,
    wave_now,
    memory,
    adjoint_now,
    adjoint_prev,
    wavelet,
    src_cells,
    src_signs,
    rec_cells,
    observed,
):
    depth, width, lanes = slowness.shape
    plane = width * lanes
    block = depth * plane
    offset = lax.axis_index("slab") * block
    decay = jnp.array(relax_decay, jnp.float32)[:, None, None, None]
    weight = jnp.array(relax_weight, jnp.float32)[:, None, None, None]
    rec_local = rec_cells - offset
    rec_inside = (rec_local >= 0) & (rec_local < block)
    rec_slot = jnp.where(rec_inside, rec_local, block)
    rec_safe = jnp.minimum(rec_slot, block - 1)
    scaled = courant / (slowness * slowness)
    older, current, relax = (wave_prev[0], wave_now[0], memory[0])
    saved = []
    misfits = []

    def record(field, level):
        picked = field.reshape(-1)[rec_safe]
        misfits.append(jnp.where(rec_inside, picked - observed[0, level], 0.0))

    src_field = place_sources(src_cells[0], src_signs[0], offset, block).reshape(
        depth, width, lanes
    )
    for level in range(STEPS):
        padded = padded_2(current, (("slab", 0),), 2)
        curved = laplace(padded)
        accel = curved + jnp.sum(relax, 0)
        newer = 2.0 * current - older + scaled * accel + wavelet[level] * src_field
        relax = decay * relax - weight * curved[None]
        older, current = (current, newer)
        saved.append(accel)
        record(current, level)
    back_prev, back_now = (adjoint_prev[0], adjoint_now[0])
    back_relax = jnp.zeros_like(relax)
    accum = jnp.zeros_like(slowness)
    for level in reversed(range(STEPS)):
        inject = (
            jnp.zeros((block,), jnp.float32)
            .at[rec_slot]
            .add(misfits[level], mode="drop")
            .reshape(depth, width, lanes)
        )
        united = back_now + inject
        pushed = scaled * united
        drive = pushed - jnp.sum(weight * back_relax, 0)
        padded = padded_2(drive, (("slab", 0),), 2)
        accum = accum + united * saved[level]
        back_prev, back_now = (-united, back_prev + 2.0 * united + laplace(padded))
        back_relax = decay * back_relax + pushed[None]
    local_grad = accum * (-2.0 * courant / (slowness * slowness * slowness))
    cells_all = lax.axis_size("slab") * block
    share = width // lax.axis_size("shot")
    first = lax.axis_index("shot") * share
    summed = lax.psum(local_grad, "shot")
    squares = lax.psum(jnp.sum(summed * summed), "slab")
    rms_value = jnp.sqrt(squares / cells_all + tiny_eps)
    normed = summed / rms_value
    new_slowness = slowness - update_rate * normed
    gradient = lax.dynamic_slice_in_dim(normed, first, share, 1)
    return (new_slowness, gradient)


def solution(mesh):
    in_specs = (
        P(("groups", "slab"), None, None),
        P(("groups", "shot"), "slab", None, None),
        P(("groups", "shot"), "slab", None, None),
        P(("groups", "shot"), None, "slab", None, None),
        P(("groups", "shot"), "slab", None, None),
        P(("groups", "shot"), "slab", None, None),
        P(),
        P(("groups", "shot"), None),
        P(("groups", "shot"), None),
        P("groups"),
        P(("groups", "shot"), None, None),
    )
    out_specs = (P(("groups", "slab"), None, None), P(("groups", "slab"), "shot", None))
    return jax.shard_map(
        per_device, mesh=mesh, in_specs=in_specs, out_specs=out_specs, check_vma=False
    )
```

profile of v0, /device:TPU:0, one launch (start us, length us, event | category | flops | bytes accessed | tf_op | source)
XLA Modules:
  0.0 167.0 jit_solution(11458838551574252018)
XLA Ops:
  7.2 1.1 slice_bitcast_fusion.1
  8.3 1.3 collective-permute-start
  9.6 5.6 %collective-permute-start.1 = (f32[2,192,128]{2,1,0:T(8,128)S(1)}, f32[2,192,128]{2,1,0:T(8,128)S(1)}, u32[]{:S(2)}, u32[]{:S(2)}) collective-permute-start(f32[2,192,128]{2,1,0:T(8,128)S(1)} %get-tuple-element.43), channel_id=1, source_target_pairs={{0,1},{1,2},{2,3},{4,5},{5,6},{6,7},{8,9},{9,10},{10,11},{12,13},{... | collective-permute-start | bytes 589832 | tf_op jit(solution)/shard_map/ppermute | solution.py:22
  15.2 0.7 convert_bitcast_fusion
  15.8 1.5 fusion.182
  17.3 0.7 fusion.166
  17.9 1.4 reduce_sum.74
  19.4 1.0 scatter_custom_fusion
  20.4 2.6 %broadcast_multiply_fusion.1 = (f32[98304]{0:T(1024)S(1)}, f32[98304]{0:T(1024)S(1)}, f32[98304]{0:T(1024)S(1)}, f32[98304]{0:T(1024)S(1)}) fusion(f32[98304]{0:T(1024)S(1)} %scatter_custom_fusion, f32[]{:T(128)} %bitcast.13, f32[]{:T(128)} %bitcast.15, f32[]{:T(128)} %bitcast.11, f32[]{:T(128)} %bitcast.5), kind=kLoop, calls=%fused_computation.281 | loop fusion | flops 393216 | bytes 1966096 | tf_op jit(solution)/shard_map/mul | solution.py:89
  23.2 1.3 fusion.155
  24.5 1.3 collective-permute-start.2
  25.8 4.6 %collective-permute-start.3 = (f32[2,192,128]{2,1,0:T(8,128)S(1)}, f32[2,192,128]{2,1,0:T(8,128)S(1)}, u32[]{:S(2)}, u32[]{:S(2)}) collective-permute-start(f32[2,192,128]{2,1,0:T(8,128)S(1)} %get-tuple-element.41), channel_id=1, source_target_pairs={{0,1},{1,2},{2,3},{4,5},{5,6},{6,7},{8,9},{9,10},{10,11},{12,13},{... | collective-permute-start | bytes 589832 | tf_op jit(solution)/shard_map/ppermute | solution.py:22
  30.4 0.2 fusion.2
  30.6 2.1 %collective-permute-done.2 = f32[2,192,128]{2,1,0:T(8,128)S(1)} collective-permute-done((f32[2,192,128]{2,1,0:T(8,128)S(1)}, f32[2,192,128]{2,1,0:T(8,128)S(1)}, u32[]{:S(2)}, u32[]{:S(2)}) %collective-permute-start.2) | collective-permute-done | bytes 196640 | tf_op jit(solution)/shard_map/ppermute | solution.py:25
  32.7 1.2 collective-permute-done.3
  33.9 0.5 add_add_fusion.2
  34.5 1.3 collective-permute-start.4
  35.8 5.0 %collective-permute-start.5 = (f32[2,192,128]{2,1,0:T(8,128)S(1)}, f32[2,192,128]{2,1,0:T(8,128)S(1)}, u32[]{:S(2)}, u32[]{:S(2)}) collective-permute-start(f32[2,192,128]{2,1,0:T(8,128)S(1)} %get-tuple-element.35), channel_id=1, source_target_pairs={{0,1},{1,2},{2,3},{4,5},{5,6},{6,7},{8,9},{9,10},{10,11},{12,13},{... | collective-permute-start | bytes 589832 | tf_op jit(solution)/shard_map/ppermute | solution.py:22
  40.8 0.6 fusion.181
  41.4 1.1 collective-permute-done.4
  42.5 1.5 collective-permute-done.5
  44.0 0.5 fusion.52
  44.5 0.5 fusion.1
  45.0 0.2 add_add_fusion.1
  45.2 0.8 fusion.178
  45.9 1.3 collective-permute-start.6
  47.2 5.0 %collective-permute-start.7 = (f32[2,192,128]{2,1,0:T(8,128)}, f32[2,192,128]{2,1,0:T(8,128)S(1)}, u32[]{:S(2)}, u32[]{:S(2)}) collective-permute-start(f32[2,192,128]{2,1,0:T(8,128)} %get-tuple-element.33), channel_id=1, source_target_pairs={{0,1},{1,2},{2,3},{4,5},{5,6},{6,7},{8,9},{9,10},{10,11},{12,13},{... | collective-permute-start | bytes 589832 | tf_op jit(solution)/shard_map/ppermute | solution.py:22
  52.3 0.6 compare_select_fusion.1
  52.8 2.3 %gather_fusion.3 = f32[256]{0:T(256)} fusion(f32[98304]{0:T(1024)S(1)} %bitcast.58, s32[1024]{0:T(1024)S(1)} %pad_clamp_fusion), kind=kCustom, calls=%fused_computation.3 | custom fusion | bytes 3072 | tf_op jit(solution)/shard_map/gather | solution.py:79
  55.2 2.3 %gather_fusion.2 = f32[256]{0:T(256)} fusion(f32[98304]{0:T(1024)S(1)} %bitcast.57, s32[1024]{0:T(1024)S(1)} %pad_clamp_fusion), kind=kCustom, calls=%fused_computation.2 | custom fusion | bytes 3072 | tf_op jit(solution)/shard_map/gather | solution.py:79
  57.5 2.3 %gather_fusion.1 = f32[256]{0:T(256)} fusion(f32[98304]{0:T(1024)S(1)} %bitcast.59, s32[1024]{0:T(1024)S(1)} %pad_clamp_fusion), kind=kCustom, calls=%fused_computation.1 | custom fusion | bytes 3072 | tf_op jit(solution)/shard_map/gather | solution.py:79
  59.8 0.7 copy-done.6
  60.5 1.6 add_add_fusion
  62.2 1.7 %gather_fusion = f32[256]{0:T(256)S(1)} fusion(f32[98304]{0:T(1024)S(1)} %bitcast.61, s32[1024]{0:T(1024)S(1)} %pad_clamp_fusion), kind=kCustom, calls=%fused_computation | custom fusion | bytes 3072 | tf_op jit(solution)/shard_map/gather | solution.py:79
  63.9 1.3 subtract_select_fusion.1
  65.2 2.2 %scatter_custom_fusion.1 = f32[98304]{0:T(1024)S(1)} fusion(s32[256]{0:T(256)} %compare_select_fusion.1, f32[256]{0:T(256)S(1)} %get-tuple-element.51, f32[]{:T(128)} %constant.19.clone.1), kind=kCustom, calls=%fused_computation.292 | custom fusion | flops 256 | bytes 393728 | tf_op jit(solution)/shard_map/scatter-add | solution.py:101
  67.4 0.1 fusion.168
  67.5 0.8 fusion.177
  68.3 1.3 collective-permute-start.8
  69.6 4.6 %collective-permute-start.9 = (f32[2,192,128]{2,1,0:T(8,128)}, f32[2,192,128]{2,1,0:T(8,128)S(1)}, u32[]{:S(2)}, u32[]{:S(2)}) collective-permute-start(f32[2,192,128]{2,1,0:T(8,128)} %get-tuple-element.31), channel_id=1, source_target_pairs={{0,1},{1,2},{2,3},{4,5},{5,6},{6,7},{8,9},{9,10},{10,11},{12,13},{... | collective-permute-start | bytes 589832 | tf_op jit(solution)/shard_map/ppermute | solution.py:22
  74.1 2.2 %scatter_custom_fusion.2 = f32[98304]{0:T(1024)S(1)} fusion(s32[256]{0:T(256)} %compare_select_fusion.1, f32[256]{0:T(256)} %get-tuple-element.50, f32[]{:T(128)} %constant.19.clone.1), kind=kCustom, calls=%fused_computation.290 | custom fusion | flops 256 | bytes 393728 | tf_op jit(solution)/shard_map/scatter-add | solution.py:101
  76.3 1.3 collective-permute-done.9
  77.6 0.7 copy-done.11
  78.3 1.6 fusion.167
  79.9 1.1 multiply_reduce_fusion.1
  81.0 0.1 fusion.169
  81.1 1.3 collective-permute-start.10
  82.4 4.9 %collective-permute-start.11 = (f32[2,192,128]{2,1,0:T(8,128)S(1)}, f32[2,192,128]{2,1,0:T(8,128)S(1)}, u32[]{:S(2)}, u32[]{:S(2)}) collective-permute-start(f32[2,192,128]{2,1,0:T(8,128)S(1)} %get-tuple-element.29), channel_id=1, source_target_pairs={{0,1},{1,2},{2,3},{4,5},{5,6},{6,7},{8,9},{9,10},{10,11},{12,13},{... | collective-permute-start | bytes 589832 | tf_op jit(solution)/shard_map/ppermute | solution.py:22
  87.3 2.8 %scatter_custom_fusion.3 = f32[98304]{0:T(1024)} fusion(s32[256]{0:T(256)} %compare_select_fusion.1, f32[256]{0:T(256)} %get-tuple-element.48, f32[]{:T(128)} %constant.19.clone.1), kind=kCustom, calls=%fused_computation.288 | custom fusion | flops 256 | bytes 393728 | tf_op jit(solution)/shard_map/scatter-add | solution.py:101
  90.2 0.3 collective-permute-done.11
  90.5 0.4 copy-done.8
  90.9 0.3 copy-done.10
  91.2 1.8 %multiply_subtract_fusion.2 = (f32[4,192,128]{2,1,0:T(8,128)S(1)}, f32[4,192,128]{2,1,0:T(8,128)S(1)}) fusion(f32[4,192,128]{2,1,0:T(8,128)} %get-tuple-element.5, f32[4,192,128]{2,1,0:T(8,128)S(1)} %copy-done, f32[4,192,128]{2,1,0:T(8,128)} %bitcast.66, f32[4,192,128]{2,1,0:T(8,128)S(1)} %fusion.169, f32[2,192,128]{2,1,0:T(8,128)} %copy-done.10, ...), kind=kLoop, calls=%fused_computation.275 | loop fusion | flops 3145728 | bytes 3538944 | tf_op jit(solution)/shard_map/sub | solution.py:106
  93.0 0.8 fusion.175
  93.8 1.3 collective-permute-start.12
  95.1 5.7 %collective-permute-start.13 = (f32[2,192,128]{2,1,0:T(8,128)}, f32[2,192,128]{2,1,0:T(8,128)}, u32[]{:S(2)}, u32[]{:S(2)}) collective-permute-start(f32[2,192,128]{2,1,0:T(8,128)} %get-tuple-element.27), channel_id=1, source_target_pairs={{0,1},{1,2},{2,3},{4,5},{5,6},{6,7},{8,9},{9,10},{10,11},{12,13},{... | collective-permute-start | bytes 589832 | tf_op jit(solution)/shard_map/ppermute | solution.py:22
  100.8 2.2 %scatter_custom_fusion.4 = f32[98304]{0:T(1024)S(1)} fusion(s32[256]{0:T(256)} %compare_select_fusion.1, f32[256]{0:T(256)S(1)} %get-tuple-element.49, f32[]{:T(128)} %constant.19.clone.1), kind=kCustom, calls=%fused_computation.286 | custom fusion | flops 256 | bytes 393728 | tf_op jit(solution)/shard_map/scatter-add | solution.py:101
  103.0 0.6 collective-permute-done.13
  103.6 2.6 %fusion.4 = f32[4,192,128]{2,1,0:T(8,128)} fusion(f32[4,192,128]{2,1,0:T(8,128)S(1)} %copy-done, f32[4,192,128]{2,1,0:T(8,128)} %get-tuple-element.24, f32[4,192,128]{2,1,0:T(8,128)S(1)} %bitcast.65, f32[2,192,128]{2,1,0:T(8,128)} %collective-permute-done.13, f32[4,192,128]{2,1,0:T(8,128)S(1)} %get-tuple-element.8, ...), kind=kLoop, calls=%fused_computation.104 | loop fusion | flops 3833856 | bytes 4718592 | tf_op jit(solution)/shard_map/mul | solution.py:111
  106.2 36.8 %all-reduce.9.cloned.1.call-done = f32[4,192,128]{2,1,0:T(8,128)} async-done(((f32[4,192,128]{2,1,0:T(8,128)}), f32[4,192,128]{2,1,0:T(8,128)}) %all-reduce.9.cloned.1.call-update) | async-done | bytes 393232 | tf_op jit(solution)/shard_map/psum | solution.py:115
  143.0 1.7 %multiply_reduce_fusion.2 = f32[]{:T(128)} fusion(f32[4,192,128]{2,1,0:T(8,128)} %all-reduce.9.cloned.1.call-done), kind=kLoop, calls=%fused_computation.274 | loop fusion | flops 196607 | bytes 393220 | tf_op jit(solution)/shard_map/reduce_sum | solution.py:116
  144.7 12.3 %psum.15 = f32[]{:T(128)} all-reduce(f32[]{:T(128)} %multiply_reduce_fusion.2), channel_id=1, replica_groups=mesh['groups'=2,'shot'=4,'slab'=4] {'slab'}, use_global_device_ids=true, to_apply=%region_14.15 | all-reduce | flops 1 | bytes 8 | tf_op jit(solution)/shard_map/psum | solution.py:116
  157.7 1.8 %multiply_subtract_fusion.1 = (f32[4,192,128]{2,1,0:T(8,128)}, f32[4,192,128]{2,1,0:T(8,128)S(1)}) fusion(f32[4,192,128]{2,1,0:T(8,128)S(1)} %copy-done, f32[4,192,128]{2,1,0:T(8,128)} %all-reduce.9.cloned.1.call-done, f32[]{:T(128)S(6)} %sqrt.3), kind=kLoop, calls=%fused_computation.273 | loop fusion | flops 294912 | bytes 1572868 | tf_op jit(solution)/shard_map/sub | solution.py:119
  159.5 0.6 constant_dynamic-slice_fusion
  (44 shorter events, 0.3 us)
Async XLA Ops:
  7.2 135.9 %all-reduce.9.cloned.1.call-start = ((), (), s32[]{:S(2)}) async-start(), calls=%async_computation | async-start | bytes 786432 | tf_op jit(solution)/shard_map/psum | solution.py:115
  8.3 14.8 %collective-permute-start = (f32[2,192,128]{2,1,0:T(8,128)S(1)}, f32[2,192,128]{2,1,0:T(8,128)S(1)}, u32[]{:S(2)}, u32[]{:S(2)}) collective-permute-start(f32[2,192,128]{2,1,0:T(8,128)S(1)} %get-tuple-element.42), channel_id=1, source_target_pairs={{1,0},{2,1},{3,2},{5,4},{6,5},{7,6},{9,8},{10,9},{11,10},{13,12},{... | collective-permute-start | bytes 589832 | tf_op jit(solution)/shard_map/ppermute | solution.py:25
  9.6 13.5 %collective-permute-start.1 = (f32[2,192,128]{2,1,0:T(8,128)S(1)}, f32[2,192,128]{2,1,0:T(8,128)S(1)}, u32[]{:S(2)}, u32[]{:S(2)}) collective-permute-start(f32[2,192,128]{2,1,0:T(8,128)S(1)} %get-tuple-element.43), channel_id=1, source_target_pairs={{0,1},{1,2},{2,3},{4,5},{5,6},{6,7},{8,9},{9,10},{10,11},{12,13},{... | collective-permute-start | bytes 589832 | tf_op jit(solution)/shard_map/ppermute | solution.py:22
  19.3 3.7 %copy-start.14 = (s32[256]{0:T(256)S(1)}, s32[256]{0:T(256)}, u32[]{:S(2)}) copy-start(s32[256]{0:T(256)} %param.22) | copy-start | bytes 3076
  19.3 3.8 %copy-start = (f32[4,192,128]{2,1,0:T(8,128)S(1)}, f32[4,192,128]{2,1,0:T(8,128)}, u32[]{:S(2)}) copy-start(f32[4,192,128]{2,1,0:T(8,128)} %param.13) | copy-start | bytes 1179652
  19.4 3.8 %copy-start.2 = (f32[1,4,192,128]{3,2,1,0:T(8,128)S(1)}, f32[1,4,192,128]{3,2,1,0:T(8,128)}, u32[]{:S(2)}) copy-start(f32[1,4,192,128]{3,2,1,0:T(8,128)} %param.15) | copy-start | bytes 1179652
  19.4 3.8 %copy-start.5 = (f32[1,4,192,128]{3,2,1,0:T(8,128)S(1)}, f32[1,4,192,128]{3,2,1,0:T(8,128)}, u32[]{:S(2)}) copy-start(f32[1,4,192,128]{3,2,1,0:T(8,128)} %param.14) | copy-start | bytes 1179652
  23.1 7.2 %copy-start.1 = (f32[1,3,4,192,128]{4,3,2,1,0:T(8,128)S(1)}, f32[1,3,4,192,128]{4,3,2,1,0:T(8,128)}, u32[]{:S(2)}) copy-start(f32[1,3,4,192,128]{4,3,2,1,0:T(8,128)} %param.16) | copy-start | bytes 3538948
  23.1 7.2 %copy-start.12 = (f32[3]{0:T(128)S(1)}, f32[3]{0:T(128)}, u32[]{:S(2)}) copy-start(f32[3]{0:T(128)} %constant.18.clone) | copy-start | bytes 40
  23.2 7.2 %copy-start.13 = (f32[3]{0:T(128)S(1)}, f32[3]{0:T(128)}, u32[]{:S(2)}) copy-start(f32[3]{0:T(128)} %constant.50.clone) | copy-start | bytes 40
  24.5 8.3 %collective-permute-start.2 = (f32[2,192,128]{2,1,0:T(8,128)S(1)}, f32[2,192,128]{2,1,0:T(8,128)S(1)}, u32[]{:S(2)}, u32[]{:S(2)}) collective-permute-start(f32[2,192,128]{2,1,0:T(8,128)S(1)} %get-tuple-element.40), channel_id=1, source_target_pairs={{1,0},{2,1},{3,2},{5,4},{6,5},{7,6},{9,8},{10,9},{11,10},{13,12},{... | collective-permute-start | bytes 589832 | tf_op jit(solution)/shard_map/ppermute | solution.py:25
  25.8 8.1 %collective-permute-start.3 = (f32[2,192,128]{2,1,0:T(8,128)S(1)}, f32[2,192,128]{2,1,0:T(8,128)S(1)}, u32[]{:S(2)}, u32[]{:S(2)}) collective-permute-start(f32[2,192,128]{2,1,0:T(8,128)S(1)} %get-tuple-element.41), channel_id=1, source_target_pairs={{0,1},{1,2},{2,3},{4,5},{5,6},{6,7},{8,9},{9,10},{10,11},{12,13},{... | collective-permute-start | bytes 589832 | tf_op jit(solution)/shard_map/ppermute | solution.py:22
  33.9 6.9 %copy-start.16 = (f32[1,4,256]{2,1,0:T(4,128)S(1)}, f32[1,4,256]{2,1,0:T(4,128)}, u32[]{:S(2)}) copy-start(f32[1,4,256]{2,1,0:T(4,128)} %param.23) | copy-start | bytes 12292
  34.5 8.0 %collective-permute-start.4 = (f32[2,192,128]{2,1,0:T(8,128)S(1)}, f32[2,192,128]{2,1,0:T(8,128)S(1)}, u32[]{:S(2)}, u32[]{:S(2)}) collective-permute-start(f32[2,192,128]{2,1,0:T(8,128)S(1)} %get-tuple-element.34), channel_id=1, source_target_pairs={{1,0},{2,1},{3,2},{5,4},{6,5},{7,6},{9,8},{10,9},{11,10},{13,12},{... | collective-permute-start | bytes 589832 | tf_op jit(solution)/shard_map/ppermute | solution.py:25
  35.8 8.2 %collective-permute-start.5 = (f32[2,192,128]{2,1,0:T(8,128)S(1)}, f32[2,192,128]{2,1,0:T(8,128)S(1)}, u32[]{:S(2)}, u32[]{:S(2)}) collective-permute-start(f32[2,192,128]{2,1,0:T(8,128)S(1)} %get-tuple-element.35), channel_id=1, source_target_pairs={{0,1},{1,2},{2,3},{4,5},{5,6},{6,7},{8,9},{9,10},{10,11},{12,13},{... | collective-permute-start | bytes 589832 | tf_op jit(solution)/shard_map/ppermute | solution.py:22
  45.0 7.3 %copy-start.15 = (s32[256]{0:T(256)S(1)}, s32[256]{0:T(256)}, u32[]{:S(2)}) copy-start(s32[256]{0:T(256)} %param.22) | copy-start | bytes 3076
  45.9 13.8 %collective-permute-start.6 = (f32[2,192,128]{2,1,0:T(8,128)}, f32[2,192,128]{2,1,0:T(8,128)S(1)}, u32[]{:S(2)}, u32[]{:S(2)}) collective-permute-start(f32[2,192,128]{2,1,0:T(8,128)} %get-tuple-element.32), channel_id=1, source_target_pairs={{1,0},{2,1},{3,2},{5,4},{6,5},{7,6},{9,8},{10,9},{11,10},{13,12},{... | collective-permute-start | bytes 589832 | tf_op jit(solution)/shard_map/ppermute | solution.py:25
  47.2 12.5 %collective-permute-start.7 = (f32[2,192,128]{2,1,0:T(8,128)}, f32[2,192,128]{2,1,0:T(8,128)S(1)}, u32[]{:S(2)}, u32[]{:S(2)}) collective-permute-start(f32[2,192,128]{2,1,0:T(8,128)} %get-tuple-element.33), channel_id=1, source_target_pairs={{0,1},{1,2},{2,3},{4,5},{5,6},{6,7},{8,9},{9,10},{10,11},{12,13},{... | collective-permute-start | bytes 589832 | tf_op jit(solution)/shard_map/ppermute | solution.py:22
  59.8 0.7 copy-start.6
  59.8 0.7 copy-start.7
  62.2 5.2 %copy-start.4 = (f32[1,4,192,128]{3,2,1,0:T(8,128)S(1)}, f32[1,4,192,128]{3,2,1,0:T(8,128)}, u32[]{:S(2)}) copy-start(f32[1,4,192,128]{3,2,1,0:T(8,128)} %param.17) | copy-start | bytes 1179652
  67.4 10.9 %copy-start.3 = (f32[1,4,192,128]{3,2,1,0:T(8,128)S(1)}, f32[1,4,192,128]{3,2,1,0:T(8,128)}, u32[]{:S(2)}) copy-start(f32[1,4,192,128]{3,2,1,0:T(8,128)} %param.18) | copy-start | bytes 1179652
  68.3 8.1 %collective-permute-start.8 = (f32[2,192,128]{2,1,0:T(8,128)}, f32[2,192,128]{2,1,0:T(8,128)S(1)}, u32[]{:S(2)}, u32[]{:S(2)}) collective-permute-start(f32[2,192,128]{2,1,0:T(8,128)} %get-tuple-element.30), channel_id=1, source_target_pairs={{1,0},{2,1},{3,2},{5,4},{6,5},{7,6},{9,8},{10,9},{11,10},{13,12},{... | collective-permute-start | bytes 589832 | tf_op jit(solution)/shard_map/ppermute | solution.py:25
  69.6 8.0 %collective-permute-start.9 = (f32[2,192,128]{2,1,0:T(8,128)}, f32[2,192,128]{2,1,0:T(8,128)S(1)}, u32[]{:S(2)}, u32[]{:S(2)}) collective-permute-start(f32[2,192,128]{2,1,0:T(8,128)} %get-tuple-element.31), channel_id=1, source_target_pairs={{0,1},{1,2},{2,3},{4,5},{5,6},{6,7},{8,9},{9,10},{10,11},{12,13},{... | collective-permute-start | bytes 589832 | tf_op jit(solution)/shard_map/ppermute | solution.py:22
  76.3 1.3 copy-start.9
  77.6 0.7 copy-start.11
  81.1 9.1 %collective-permute-start.10 = (f32[2,192,128]{2,1,0:T(8,128)S(1)}, f32[2,192,128]{2,1,0:T(8,128)S(1)}, u32[]{:S(2)}, u32[]{:S(2)}) collective-permute-start(f32[2,192,128]{2,1,0:T(8,128)S(1)} %get-tuple-element.28), channel_id=1, source_target_pairs={{1,0},{2,1},{3,2},{5,4},{6,5},{7,6},{9,8},{10,9},{11,10},{13,12},{... | collective-permute-start | bytes 589832 | tf_op jit(solution)/shard_map/ppermute | solution.py:25
  82.4 8.1 %collective-permute-start.11 = (f32[2,192,128]{2,1,0:T(8,128)S(1)}, f32[2,192,128]{2,1,0:T(8,128)S(1)}, u32[]{:S(2)}, u32[]{:S(2)}) collective-permute-start(f32[2,192,128]{2,1,0:T(8,128)S(1)} %get-tuple-element.29), channel_id=1, source_target_pairs={{0,1},{1,2},{2,3},{4,5},{5,6},{6,7},{8,9},{9,10},{10,11},{12,13},{... | collective-permute-start | bytes 589832 | tf_op jit(solution)/shard_map/ppermute | solution.py:22
  90.2 0.7 copy-start.8
  90.5 0.7 copy-start.10
  93.8 9.2 %collective-permute-start.12 = (f32[2,192,128]{2,1,0:T(8,128)}, f32[2,192,128]{2,1,0:T(8,128)}, u32[]{:S(2)}, u32[]{:S(2)}) collective-permute-start(f32[2,192,128]{2,1,0:T(8,128)} %get-tuple-element.26), channel_id=1, source_target_pairs={{1,0},{2,1},{3,2},{5,4},{6,5},{7,6},{9,8},{10,9},{11,10},{13,12},{... | collective-permute-start | bytes 589832 | tf_op jit(solution)/shard_map/ppermute | solution.py:25
  95.1 8.5 %collective-permute-start.13 = (f32[2,192,128]{2,1,0:T(8,128)}, f32[2,192,128]{2,1,0:T(8,128)}, u32[]{:S(2)}, u32[]{:S(2)}) collective-permute-start(f32[2,192,128]{2,1,0:T(8,128)} %get-tuple-element.27), channel_id=1, source_target_pairs={{0,1},{1,2},{2,3},{4,5},{5,6},{6,7},{8,9},{9,10},{10,11},{12,13},{... | collective-permute-start | bytes 589832 | tf_op jit(solution)/shard_map/ppermute | solution.py:22
Sparse Core Ops, SparseCore 0:
  106.3 36.6 all-reduce.8
where the time goes:
time: 168 us; the launch traced here: 167 us
  waiting for transfers between devices  44.9 us (27%)
  starting transfers between devices  44.4 us (26%)
  other arithmetic  33.3 us (20%)
  local copies, waits for them, and re-layouts  17 us (10%)
  between operations  15.2 us (9%)
  blocking collectives  12.3 us (7%)
    psum x1, waiting for transfers between devices, per_device(): summed = lax.psum(local_grad, 'shot')  36.8 us
    ppermute x7, starting transfers between devices, padded_2(): lax.ppermute(lax.slice_in_dim(block, block.shape[dim] - width, None, axis...  35.4 us
    psum x1, blocking collectives, per_device(): squares = lax.psum(jnp.sum(summed * summed), 'slab')  12.3 us
    scatter-add x4, other arithmetic, per_device(): inject = jnp.zeros((block,), jnp.float32).at[rec_slot].add(misfits[level]...  9.37 us
    ppermute x7, starting transfers between devices, padded_2(): lax.ppermute(lax.slice_in_dim(block, 0, width, axis=dim), axis, backward)  9.01 us
    gather x4, local copies, waits for them, and re-layouts, record(): picked = field.reshape(-1)[rec_safe]  8.65 us
    ppermute x7, waiting for transfers between devices, padded_2(): lax.ppermute(lax.slice_in_dim(block, block.shape[dim] - width, None, axis...  4.85 us
    add x4, other arithmetic, per_device(): newer = 2.0 * current - older + scaled * accel + wavelet[level] * src_field  3.63 us
  transfers between devices with their start and end apart: 15, of which 8 were waited for; matrix products, arithmetic and copies ran while one was open for 14% of the time, Pallas kernels for 0%

commit v1 on v0

--- a/solution.py
+++ b/solution.py
@@ -112,7 +112,9 @@
     cells_all = lax.axis_size("slab") * block
     share = width // lax.axis_size("shot")
     first = lax.axis_index("shot") * share
-    summed = lax.psum(local_grad, "shot")
+    summed = local_grad
+    for hop in (1, 2):
+        summed = summed + lax.ppermute(summed, "shot", [(dev, dev ^ hop) for dev in range(4)])
     squares = lax.psum(jnp.sum(summed * summed), "slab")
     rms_value = jnp.sqrt(squares / cells_all + tiny_eps)
     normed = summed / rms_value

time: 168 us -> 131 us (0.78)
  waiting for transfers between devices: 44.9 us -> 19.3 us
  between operations: 15.2 us -> 1.79 us
  other arithmetic: 33.3 us -> 30.5 us
  blocking collectives: 12.3 us -> 15 us
  starting transfers between devices: 44.4 us -> 46.2 us
    psum x1 -> x0, waiting for transfers between devices: 36.8 us -> none  [per_device(): summed = lax.psum(local_grad, 'shot')]
    ppermute x0 -> x2, waiting for transfers between devices: none -> 11.2 us  [per_device(): lax.ppermute(summed, 'shot', [(dev, dev ^ hop) for dev in range(4)])]
    psum x1, blocking collectives: 12.3 us -> 15 us  [per_device(): squares = lax.psum(jnp.sum(summed * summed), 'slab')]
    ppermute x0 -> x2, starting transfers between devices: none -> 1.78 us  [per_device(): lax.ppermute(summed, 'shot', [(dev, dev ^ hop) for dev in range(4)])]
  transfers between devices with their start and end apart: 15 -> 16, of which waited for: 8 -> 9; matrix products, arithmetic and copies ran while one was open for 14% -> 18% of each run, Pallas kernels for 0% -> 0%
where the time goes in v1:
time: 131 us; the launch traced here: 130 us
  starting transfers between devices  46.2 us (35%)
  other arithmetic  30.5 us (23%)
  waiting for transfers between devices  19.3 us (15%)
  local copies, waits for them, and re-layouts  17 us (13%)
  blocking collectives  15 us (11%)
  between operations  1.79 us (1%)
    ppermute x7, starting transfers between devices, padded_2(): lax.ppermute(lax.slice_in_dim(block, block.shape[dim] - width, None, axis...  35.4 us
    psum x1, blocking collectives, per_device(): squares = lax.psum(jnp.sum(summed * summed), 'slab')  15 us
    ppermute x2, waiting for transfers between devices, per_device(): lax.ppermute(summed, 'shot', [(dev, dev ^ hop) for dev in range(4)])  11.2 us
    scatter-add x4, other arithmetic, per_device(): inject = jnp.zeros((block,), jnp.float32).at[rec_slot].add(misfits[level]...  9.35 us
    ppermute x7, starting transfers between devices, padded_2(): lax.ppermute(lax.slice_in_dim(block, 0, width, axis=dim), axis, backward)  9.01 us
    gather x4, local copies, waits for them, and re-layouts, record(): picked = field.reshape(-1)[rec_safe]  8.69 us
    ppermute x7, waiting for transfers between devices, padded_2(): lax.ppermute(lax.slice_in_dim(block, block.shape[dim] - width, None, axis...  4.87 us
    add x4, other arithmetic, per_device(): newer = 2.0 * current - older + scaled * accel + wavelet[level] * src_field  3.63 us
  transfers between devices with their start and end apart: 16, of which 9 were waited for; matrix products, arithmetic and copies ran while one was open for 18% of the time, Pallas kernels for 0%

profile of v1, /device:TPU:0, one launch (start us, length us, event | category | flops | bytes accessed | tf_op | source)
XLA Modules:
  0.0 129.8 jit_solution(16587008127004267591)
XLA Ops:
  0.6 1.1 slice_bitcast_fusion.1
  1.7 1.3 collective-permute-start
  3.0 5.6 %collective-permute-start.1 = (f32[2,192,128]{2,1,0:T(8,128)S(1)}, f32[2,192,128]{2,1,0:T(8,128)S(1)}, u32[]{:S(2)}, u32[]{:S(2)}) collective-permute-start(f32[2,192,128]{2,1,0:T(8,128)S(1)} %get-tuple-element.45), channel_id=1, source_target_pairs={{0,1},{1,2},{2,3},{4,5},{5,6},{6,7},{8,9},{9,10},{10,11},{12,13},{... | collective-permute-start | bytes 589832 | tf_op jit(solution)/shard_map/ppermute | solution.py:22
  8.6 0.7 convert_bitcast_fusion
  9.3 1.5 %fusion.182 = (f32[1]{0:T(128)}, f32[1]{0:T(128)}, f32[1]{0:T(128)}, f32[1]{0:T(128)}) fusion(f32[4]{0:T(128)} %param.19), kind=kLoop, calls=%fused_computation.320 | loop fusion | bytes 32 | tf_op jit(solution)/shard_map/slice | solution.py:89
  10.7 0.7 fusion.166
  11.4 1.4 %reduce_sum.74 = f32[4,192,128]{2,1,0:T(8,128)S(1)} reduce(f32[1,3,4,192,128]{4,3,2,1,0:T(8,128)} %param.16, f32[]{:T(128)} %constant.19.clone.1), dimensions={0,1}, to_apply=%region_0.1 | reduce | flops 196608 | bytes 1572868 | tf_op jit(solution)/shard_map/reduce_sum | solution.py:88
  12.8 1.0 scatter_custom_fusion
  13.8 2.6 %broadcast_multiply_fusion.1 = (f32[98304]{0:T(1024)S(1)}, f32[98304]{0:T(1024)S(1)}, f32[98304]{0:T(1024)S(1)}, f32[98304]{0:T(1024)S(1)}) fusion(f32[98304]{0:T(1024)S(1)} %scatter_custom_fusion, f32[]{:T(128)} %bitcast.13, f32[]{:T(128)} %bitcast.15, f32[]{:T(128)} %bitcast.11, f32[]{:T(128)} %bitcast.5), kind=kLoop, calls=%fused_computation.281 | loop fusion | flops 393216 | bytes 1966096 | tf_op jit(solution)/shard_map/mul | solution.py:89
  16.6 1.3 fusion.155
  17.9 1.3 collective-permute-start.2
  19.2 4.6 %collective-permute-start.3 = (f32[2,192,128]{2,1,0:T(8,128)S(1)}, f32[2,192,128]{2,1,0:T(8,128)S(1)}, u32[]{:S(2)}, u32[]{:S(2)}) collective-permute-start(f32[2,192,128]{2,1,0:T(8,128)S(1)} %get-tuple-element.43), channel_id=1, source_target_pairs={{0,1},{1,2},{2,3},{4,5},{5,6},{6,7},{8,9},{9,10},{10,11},{12,13},{... | collective-permute-start | bytes 589832 | tf_op jit(solution)/shard_map/ppermute | solution.py:22
  23.8 0.2 fusion.2
  24.1 2.1 %collective-permute-done.2 = f32[2,192,128]{2,1,0:T(8,128)S(1)} collective-permute-done((f32[2,192,128]{2,1,0:T(8,128)S(1)}, f32[2,192,128]{2,1,0:T(8,128)S(1)}, u32[]{:S(2)}, u32[]{:S(2)}) %collective-permute-start.2) | collective-permute-done | bytes 196640 | tf_op jit(solution)/shard_map/ppermute | solution.py:25
  26.2 1.2 collective-permute-done.3
  27.3 0.5 add_add_fusion.2
  27.9 1.3 collective-permute-start.4
  29.2 5.0 %collective-permute-start.5 = (f32[2,192,128]{2,1,0:T(8,128)S(1)}, f32[2,192,128]{2,1,0:T(8,128)S(1)}, u32[]{:S(2)}, u32[]{:S(2)}) collective-permute-start(f32[2,192,128]{2,1,0:T(8,128)S(1)} %get-tuple-element.37), channel_id=1, source_target_pairs={{0,1},{1,2},{2,3},{4,5},{5,6},{6,7},{8,9},{9,10},{10,11},{12,13},{... | collective-permute-start | bytes 589832 | tf_op jit(solution)/shard_map/ppermute | solution.py:22
  34.3 0.6 fusion.181
  34.9 1.1 collective-permute-done.4
  35.9 1.5 %collective-permute-done.5 = f32[2,192,128]{2,1,0:T(8,128)S(1)} collective-permute-done((f32[2,192,128]{2,1,0:T(8,128)S(1)}, f32[2,192,128]{2,1,0:T(8,128)S(1)}, u32[]{:S(2)}, u32[]{:S(2)}) %collective-permute-start.5) | collective-permute-done | bytes 196640 | tf_op jit(solution)/shard_map/ppermute | solution.py:22
  37.4 0.5 fusion.52
  37.9 0.5 fusion.1
  38.4 0.2 add_add_fusion.1
  38.6 0.8 fusion.178
  39.3 1.3 collective-permute-start.6
  40.6 5.0 %collective-permute-start.7 = (f32[2,192,128]{2,1,0:T(8,128)}, f32[2,192,128]{2,1,0:T(8,128)S(1)}, u32[]{:S(2)}, u32[]{:S(2)}) collective-permute-start(f32[2,192,128]{2,1,0:T(8,128)} %get-tuple-element.35), channel_id=1, source_target_pairs={{0,1},{1,2},{2,3},{4,5},{5,6},{6,7},{8,9},{9,10},{10,11},{12,13},{... | collective-permute-start | bytes 589832 | tf_op jit(solution)/shard_map/ppermute | solution.py:22
  45.7 0.6 compare_select_fusion.1
  46.2 2.3 %gather_fusion.3 = f32[256]{0:T(256)} fusion(f32[98304]{0:T(1024)S(1)} %bitcast.58, s32[1024]{0:T(1024)S(1)} %pad_clamp_fusion), kind=kCustom, calls=%fused_computation.3 | custom fusion | bytes 3072 | tf_op jit(solution)/shard_map/gather | solution.py:79
  48.6 2.3 %gather_fusion.2 = f32[256]{0:T(256)} fusion(f32[98304]{0:T(1024)S(1)} %bitcast.57, s32[1024]{0:T(1024)S(1)} %pad_clamp_fusion), kind=kCustom, calls=%fused_computation.2 | custom fusion | bytes 3072 | tf_op jit(solution)/shard_map/gather | solution.py:79
  50.9 2.3 %gather_fusion.1 = f32[256]{0:T(256)} fusion(f32[98304]{0:T(1024)S(1)} %bitcast.59, s32[1024]{0:T(1024)S(1)} %pad_clamp_fusion), kind=kCustom, calls=%fused_computation.1 | custom fusion | bytes 3072 | tf_op jit(solution)/shard_map/gather | solution.py:79
  53.2 0.7 copy-done.6
  54.0 1.6 %add_add_fusion = (f32[4,192,128]{2,1,0:T(8,128)S(1)}, f32[4,192,128]{2,1,0:T(8,128)S(1)}) fusion(f32[4,192,128]{2,1,0:T(8,128)S(1)} %bitcast.62, f32[4,192,128]{2,1,0:T(8,128)S(1)} %get-tuple-element.20, f32[4,192,128]{2,1,0:T(8,128)S(1)} %get-tuple-element.18, f32[4,192,128]{2,1,0:T(8,128)S(1)} %copy-done, f32[4,192,128]{2,1,0:T(8,128)S(1)} %get-tuple-element.3, ...), kind=kLoop, calls=%fused_computation.276 | loop fusion | flops 3047424 | bytes 3145728 | tf_op jit(solution)/shard_map/add | solution.py:89
  55.6 1.7 %gather_fusion = f32[256]{0:T(256)S(1)} fusion(f32[98304]{0:T(1024)S(1)} %bitcast.61, s32[1024]{0:T(1024)S(1)} %pad_clamp_fusion), kind=kCustom, calls=%fused_computation | custom fusion | bytes 3072 | tf_op jit(solution)/shard_map/gather | solution.py:79
  57.4 1.3 subtract_select_fusion.1
  58.6 2.2 %scatter_custom_fusion.1 = f32[98304]{0:T(1024)S(1)} fusion(s32[256]{0:T(256)} %compare_select_fusion.1, f32[256]{0:T(256)S(1)} %get-tuple-element.53, f32[]{:T(128)} %constant.19.clone.1), kind=kCustom, calls=%fused_computation.292 | custom fusion | flops 256 | bytes 393728 | tf_op jit(solution)/shard_map/scatter-add | solution.py:101
  60.9 0.8 fusion.177
  61.7 1.3 collective-permute-start.8
  63.0 4.6 %collective-permute-start.9 = (f32[2,192,128]{2,1,0:T(8,128)}, f32[2,192,128]{2,1,0:T(8,128)S(1)}, u32[]{:S(2)}, u32[]{:S(2)}) collective-permute-start(f32[2,192,128]{2,1,0:T(8,128)} %get-tuple-element.33), channel_id=1, source_target_pairs={{0,1},{1,2},{2,3},{4,5},{5,6},{6,7},{8,9},{9,10},{10,11},{12,13},{... | collective-permute-start | bytes 589832 | tf_op jit(solution)/shard_map/ppermute | solution.py:22
  67.6 2.2 %scatter_custom_fusion.2 = f32[98304]{0:T(1024)S(1)} fusion(s32[256]{0:T(256)} %compare_select_fusion.1, f32[256]{0:T(256)} %get-tuple-element.52, f32[]{:T(128)} %constant.19.clone.1), kind=kCustom, calls=%fused_computation.290 | custom fusion | flops 256 | bytes 393728 | tf_op jit(solution)/shard_map/scatter-add | solution.py:101
  69.8 1.3 collective-permute-done.9
  71.0 0.7 copy-done.11
  71.7 1.6 %fusion.167 = (f32[4,192,128]{2,1,0:T(8,128)S(1)}, f32[4,192,128]{2,1,0:T(8,128)S(1)}) fusion(f32[4,192,128]{2,1,0:T(8,128)S(1)} %copy-done, f32[4,192,128]{2,1,0:T(8,128)S(1)} %bitcast.67, f32[4,192,128]{2,1,0:T(8,128)S(1)} %get-tuple-element.14, f32[2,192,128]{2,1,0:T(8,128)} %copy-done.11, f32[2,192,128]{2,1,0:T(8,128)} %copy-done.9, ...), kind=kLoop, calls=%fused_computation.310 | loop fusion | flops 2949120 | bytes 3145728 | tf_op jit(solution)/shard_map/mul | solution.py:105
  73.3 1.1 multiply_reduce_fusion.1
  74.6 1.3 collective-permute-start.10
  75.9 4.9 %collective-permute-start.11 = (f32[2,192,128]{2,1,0:T(8,128)S(1)}, f32[2,192,128]{2,1,0:T(8,128)S(1)}, u32[]{:S(2)}, u32[]{:S(2)}) collective-permute-start(f32[2,192,128]{2,1,0:T(8,128)S(1)} %get-tuple-element.31), channel_id=1, source_target_pairs={{0,1},{1,2},{2,3},{4,5},{5,6},{6,7},{8,9},{9,10},{10,11},{12,13},{... | collective-permute-start | bytes 589832 | tf_op jit(solution)/shard_map/ppermute | solution.py:22
  80.8 2.8 %scatter_custom_fusion.3 = f32[98304]{0:T(1024)} fusion(s32[256]{0:T(256)} %compare_select_fusion.1, f32[256]{0:T(256)} %get-tuple-element.50, f32[]{:T(128)} %constant.19.clone.1), kind=kCustom, calls=%fused_computation.288 | custom fusion | flops 256 | bytes 393728 | tf_op jit(solution)/shard_map/scatter-add | solution.py:101
  83.6 0.3 collective-permute-done.11
  83.9 0.3 copy-done.8
  84.3 0.3 copy-done.10
  84.6 1.8 %multiply_subtract_fusion.2 = (f32[4,192,128]{2,1,0:T(8,128)S(1)}, f32[4,192,128]{2,1,0:T(8,128)S(1)}) fusion(f32[4,192,128]{2,1,0:T(8,128)} %get-tuple-element.5, f32[4,192,128]{2,1,0:T(8,128)S(1)} %copy-done, f32[4,192,128]{2,1,0:T(8,128)} %bitcast.66, f32[4,192,128]{2,1,0:T(8,128)S(1)} %fusion.169, f32[2,192,128]{2,1,0:T(8,128)} %copy-done.10, ...), kind=kLoop, calls=%fused_computation.275 | loop fusion | flops 3145728 | bytes 3538944 | tf_op jit(solution)/shard_map/sub | solution.py:106
  86.5 0.8 fusion.175
  87.2 1.3 collective-permute-start.12
  88.5 5.7 %collective-permute-start.13 = (f32[2,192,128]{2,1,0:T(8,128)}, f32[2,192,128]{2,1,0:T(8,128)}, u32[]{:S(2)}, u32[]{:S(2)}) collective-permute-start(f32[2,192,128]{2,1,0:T(8,128)} %get-tuple-element.29), channel_id=1, source_target_pairs={{0,1},{1,2},{2,3},{4,5},{5,6},{6,7},{8,9},{9,10},{10,11},{12,13},{... | collective-permute-start | bytes 589832 | tf_op jit(solution)/shard_map/ppermute | solution.py:22
  94.2 2.2 %scatter_custom_fusion.4 = f32[98304]{0:T(1024)S(1)} fusion(s32[256]{0:T(256)} %compare_select_fusion.1, f32[256]{0:T(256)S(1)} %get-tuple-element.51, f32[]{:T(128)} %constant.19.clone.1), kind=kCustom, calls=%fused_computation.286 | custom fusion | flops 256 | bytes 393728 | tf_op jit(solution)/shard_map/scatter-add | solution.py:101
  96.4 0.6 collective-permute-done.13
  97.0 1.9 %fusion.4 = f32[4,192,128]{2,1,0:T(8,128)S(1)} fusion(f32[4,192,128]{2,1,0:T(8,128)S(1)} %copy-done, f32[4,192,128]{2,1,0:T(8,128)} %get-tuple-element.26, f32[4,192,128]{2,1,0:T(8,128)S(1)} %bitcast.65, f32[2,192,128]{2,1,0:T(8,128)} %collective-permute-done.13, f32[4,192,128]{2,1,0:T(8,128)S(1)} %get-tuple-element.10, ...), kind=kLoop, calls=%fused_computation.104 | loop fusion | flops 3833856 | bytes 4718592 | tf_op jit(solution)/shard_map/mul | solution.py:111
  99.0 1.7 %collective-permute-done.14 = f32[4,192,128]{2,1,0:T(8,128)S(1)} collective-permute-done((f32[4,192,128]{2,1,0:T(8,128)S(1)}, f32[4,192,128]{2,1,0:T(8,128)S(1)}, u32[]{:S(2)}, u32[]{:S(2)}) %collective-permute-start.14) | collective-permute-done | bytes 393248 | tf_op jit(solution)/shard_map/ppermute | solution.py:117
  100.7 1.7 %collective-permute-start.15 = (f32[4,192,128]{2,1,0:T(8,128)S(1)}, f32[4,192,128]{2,1,0:T(8,128)S(1)}, u32[]{:S(2)}, u32[]{:S(2)}) collective-permute-start(f32[4,192,128]{2,1,0:T(8,128)S(1)} %add.519), channel_id=1, source_target_pairs={{0,8},{4,12},{8,0},{12,4},{1,9},{5,13},{9,1},{13,5},{2,10},{6,14},... | collective-permute-start | bytes 1179656 | tf_op jit(solution)/shard_map/ppermute | solution.py:117
  102.4 9.5 %collective-permute-done.15 = f32[4,192,128]{2,1,0:T(8,128)S(1)} collective-permute-done((f32[4,192,128]{2,1,0:T(8,128)S(1)}, f32[4,192,128]{2,1,0:T(8,128)S(1)}, u32[]{:S(2)}, u32[]{:S(2)}) %collective-permute-start.15) | collective-permute-done | bytes 393248 | tf_op jit(solution)/shard_map/ppermute | solution.py:117
  112.0 0.7 multiply_reduce_fusion.2
  112.7 15.0 %psum.7 = f32[]{:T(128)} all-reduce(f32[]{:T(128)} %get-tuple-element.8), channel_id=1, replica_groups=mesh['groups'=2,'shot'=4,'slab'=4] {'slab'}, use_global_device_ids=true, to_apply=%region_13.14 | all-reduce | flops 1 | bytes 8 | tf_op jit(solution)/shard_map/psum | solution.py:118
  128.4 0.8 multiply_subtract_fusion.1
  129.2 0.6 constant_dynamic-slice_fusion
  (46 shorter events, 0.5 us)
Async XLA Ops:
  1.7 14.8 %collective-permute-start = (f32[2,192,128]{2,1,0:T(8,128)S(1)}, f32[2,192,128]{2,1,0:T(8,128)S(1)}, u32[]{:S(2)}, u32[]{:S(2)}) collective-permute-start(f32[2,192,128]{2,1,0:T(8,128)S(1)} %get-tuple-element.44), channel_id=1, source_target_pairs={{1,0},{2,1},{3,2},{5,4},{6,5},{7,6},{9,8},{10,9},{11,10},{13,12},{... | collective-permute-start | bytes 589832 | tf_op jit(solution)/shard_map/ppermute | solution.py:25
  3.0 13.5 %collective-permute-start.1 = (f32[2,192,128]{2,1,0:T(8,128)S(1)}, f32[2,192,128]{2,1,0:T(8,128)S(1)}, u32[]{:S(2)}, u32[]{:S(2)}) collective-permute-start(f32[2,192,128]{2,1,0:T(8,128)S(1)} %get-tuple-element.45), channel_id=1, source_target_pairs={{0,1},{1,2},{2,3},{4,5},{5,6},{6,7},{8,9},{9,10},{10,11},{12,13},{... | collective-permute-start | bytes 589832 | tf_op jit(solution)/shard_map/ppermute | solution.py:22
  12.8 3.7 %copy-start.14 = (s32[256]{0:T(256)S(1)}, s32[256]{0:T(256)}, u32[]{:S(2)}) copy-start(s32[256]{0:T(256)} %param.22) | copy-start | bytes 3076
  12.8 3.7 %copy-start = (f32[4,192,128]{2,1,0:T(8,128)S(1)}, f32[4,192,128]{2,1,0:T(8,128)}, u32[]{:S(2)}) copy-start(f32[4,192,128]{2,1,0:T(8,128)} %param.13) | copy-start | bytes 1179652
  12.8 3.7 %copy-start.2 = (f32[1,4,192,128]{3,2,1,0:T(8,128)S(1)}, f32[1,4,192,128]{3,2,1,0:T(8,128)}, u32[]{:S(2)}) copy-start(f32[1,4,192,128]{3,2,1,0:T(8,128)} %param.15) | copy-start | bytes 1179652
  12.8 3.7 %copy-start.5 = (f32[1,4,192,128]{3,2,1,0:T(8,128)S(1)}, f32[1,4,192,128]{3,2,1,0:T(8,128)}, u32[]{:S(2)}) copy-start(f32[1,4,192,128]{3,2,1,0:T(8,128)} %param.14) | copy-start | bytes 1179652
  16.5 7.2 %copy-start.1 = (f32[1,3,4,192,128]{4,3,2,1,0:T(8,128)S(1)}, f32[1,3,4,192,128]{4,3,2,1,0:T(8,128)}, u32[]{:S(2)}) copy-start(f32[1,3,4,192,128]{4,3,2,1,0:T(8,128)} %param.16) | copy-start | bytes 3538948
  16.6 7.2 %copy-start.12 = (f32[3]{0:T(128)S(1)}, f32[3]{0:T(128)}, u32[]{:S(2)}) copy-start(f32[3]{0:T(128)} %constant.18.clone) | copy-start | bytes 40
  16.6 7.2 %copy-start.13 = (f32[3]{0:T(128)S(1)}, f32[3]{0:T(128)}, u32[]{:S(2)}) copy-start(f32[3]{0:T(128)} %constant.50.clone) | copy-start | bytes 40
  17.9 8.3 %collective-permute-start.2 = (f32[2,192,128]{2,1,0:T(8,128)S(1)}, f32[2,192,128]{2,1,0:T(8,128)S(1)}, u32[]{:S(2)}, u32[]{:S(2)}) collective-permute-start(f32[2,192,128]{2,1,0:T(8,128)S(1)} %get-tuple-element.42), channel_id=1, source_target_pairs={{1,0},{2,1},{3,2},{5,4},{6,5},{7,6},{9,8},{10,9},{11,10},{13,12},{... | collective-permute-start | bytes 589832 | tf_op jit(solution)/shard_map/ppermute | solution.py:25
  19.2 8.1 %collective-permute-start.3 = (f32[2,192,128]{2,1,0:T(8,128)S(1)}, f32[2,192,128]{2,1,0:T(8,128)S(1)}, u32[]{:S(2)}, u32[]{:S(2)}) collective-permute-start(f32[2,192,128]{2,1,0:T(8,128)S(1)} %get-tuple-element.43), channel_id=1, source_target_pairs={{0,1},{1,2},{2,3},{4,5},{5,6},{6,7},{8,9},{9,10},{10,11},{12,13},{... | collective-permute-start | bytes 589832 | tf_op jit(solution)/shard_map/ppermute | solution.py:22
  27.3 6.9 %copy-start.16 = (f32[1,4,256]{2,1,0:T(4,128)S(1)}, f32[1,4,256]{2,1,0:T(4,128)}, u32[]{:S(2)}) copy-start(f32[1,4,256]{2,1,0:T(4,128)} %param.23) | copy-start | bytes 12292
  27.9 8.0 %collective-permute-start.4 = (f32[2,192,128]{2,1,0:T(8,128)S(1)}, f32[2,192,128]{2,1,0:T(8,128)S(1)}, u32[]{:S(2)}, u32[]{:S(2)}) collective-permute-start(f32[2,192,128]{2,1,0:T(8,128)S(1)} %get-tuple-element.36), channel_id=1, source_target_pairs={{1,0},{2,1},{3,2},{5,4},{6,5},{7,6},{9,8},{10,9},{11,10},{13,12},{... | collective-permute-start | bytes 589832 | tf_op jit(solution)/shard_map/ppermute | solution.py:25
  29.2 8.2 %collective-permute-start.5 = (f32[2,192,128]{2,1,0:T(8,128)S(1)}, f32[2,192,128]{2,1,0:T(8,128)S(1)}, u32[]{:S(2)}, u32[]{:S(2)}) collective-permute-start(f32[2,192,128]{2,1,0:T(8,128)S(1)} %get-tuple-element.37), channel_id=1, source_target_pairs={{0,1},{1,2},{2,3},{4,5},{5,6},{6,7},{8,9},{9,10},{10,11},{12,13},{... | collective-permute-start | bytes 589832 | tf_op jit(solution)/shard_map/ppermute | solution.py:22
  38.4 7.3 %copy-start.15 = (s32[256]{0:T(256)S(1)}, s32[256]{0:T(256)}, u32[]{:S(2)}) copy-start(s32[256]{0:T(256)} %param.22) | copy-start | bytes 3076
  39.3 13.9 %collective-permute-start.6 = (f32[2,192,128]{2,1,0:T(8,128)}, f32[2,192,128]{2,1,0:T(8,128)S(1)}, u32[]{:S(2)}, u32[]{:S(2)}) collective-permute-start(f32[2,192,128]{2,1,0:T(8,128)} %get-tuple-element.34), channel_id=1, source_target_pairs={{1,0},{2,1},{3,2},{5,4},{6,5},{7,6},{9,8},{10,9},{11,10},{13,12},{... | collective-permute-start | bytes 589832 | tf_op jit(solution)/shard_map/ppermute | solution.py:25
  40.6 12.6 %collective-permute-start.7 = (f32[2,192,128]{2,1,0:T(8,128)}, f32[2,192,128]{2,1,0:T(8,128)S(1)}, u32[]{:S(2)}, u32[]{:S(2)}) collective-permute-start(f32[2,192,128]{2,1,0:T(8,128)} %get-tuple-element.35), channel_id=1, source_target_pairs={{0,1},{1,2},{2,3},{4,5},{5,6},{6,7},{8,9},{9,10},{10,11},{12,13},{... | collective-permute-start | bytes 589832 | tf_op jit(solution)/shard_map/ppermute | solution.py:22
  53.2 0.7 copy-start.6
  53.2 0.7 copy-start.7
  55.6 5.2 %copy-start.4 = (f32[1,4,192,128]{3,2,1,0:T(8,128)S(1)}, f32[1,4,192,128]{3,2,1,0:T(8,128)}, u32[]{:S(2)}) copy-start(f32[1,4,192,128]{3,2,1,0:T(8,128)} %param.17) | copy-start | bytes 1179652
  60.8 10.9 %copy-start.3 = (f32[1,4,192,128]{3,2,1,0:T(8,128)S(1)}, f32[1,4,192,128]{3,2,1,0:T(8,128)}, u32[]{:S(2)}) copy-start(f32[1,4,192,128]{3,2,1,0:T(8,128)} %param.18) | copy-start | bytes 1179652
  61.7 8.1 %collective-permute-start.8 = (f32[2,192,128]{2,1,0:T(8,128)}, f32[2,192,128]{2,1,0:T(8,128)S(1)}, u32[]{:S(2)}, u32[]{:S(2)}) collective-permute-start(f32[2,192,128]{2,1,0:T(8,128)} %get-tuple-element.32), channel_id=1, source_target_pairs={{1,0},{2,1},{3,2},{5,4},{6,5},{7,6},{9,8},{10,9},{11,10},{13,12},{... | collective-permute-start | bytes 589832 | tf_op jit(solution)/shard_map/ppermute | solution.py:25
  63.0 8.0 %collective-permute-start.9 = (f32[2,192,128]{2,1,0:T(8,128)}, f32[2,192,128]{2,1,0:T(8,128)S(1)}, u32[]{:S(2)}, u32[]{:S(2)}) collective-permute-start(f32[2,192,128]{2,1,0:T(8,128)} %get-tuple-element.33), channel_id=1, source_target_pairs={{0,1},{1,2},{2,3},{4,5},{5,6},{6,7},{8,9},{9,10},{10,11},{12,13},{... | collective-permute-start | bytes 589832 | tf_op jit(solution)/shard_map/ppermute | solution.py:22
  69.8 1.3 copy-start.9
  71.0 0.7 copy-start.11
  74.6 9.0 %collective-permute-start.10 = (f32[2,192,128]{2,1,0:T(8,128)S(1)}, f32[2,192,128]{2,1,0:T(8,128)S(1)}, u32[]{:S(2)}, u32[]{:S(2)}) collective-permute-start(f32[2,192,128]{2,1,0:T(8,128)S(1)} %get-tuple-element.30), channel_id=1, source_target_pairs={{1,0},{2,1},{3,2},{5,4},{6,5},{7,6},{9,8},{10,9},{11,10},{13,12},{... | collective-permute-start | bytes 589832 | tf_op jit(solution)/shard_map/ppermute | solution.py:25
  75.9 8.1 %collective-permute-start.11 = (f32[2,192,128]{2,1,0:T(8,128)S(1)}, f32[2,192,128]{2,1,0:T(8,128)S(1)}, u32[]{:S(2)}, u32[]{:S(2)}) collective-permute-start(f32[2,192,128]{2,1,0:T(8,128)S(1)} %get-tuple-element.31), channel_id=1, source_target_pairs={{0,1},{1,2},{2,3},{4,5},{5,6},{6,7},{8,9},{9,10},{10,11},{12,13},{... | collective-permute-start | bytes 589832 | tf_op jit(solution)/shard_map/ppermute | solution.py:22
  83.6 0.7 copy-start.8
  83.9 0.7 copy-start.10
  87.2 9.2 %collective-permute-start.12 = (f32[2,192,128]{2,1,0:T(8,128)}, f32[2,192,128]{2,1,0:T(8,128)}, u32[]{:S(2)}, u32[]{:S(2)}) collective-permute-start(f32[2,192,128]{2,1,0:T(8,128)} %get-tuple-element.28), channel_id=1, source_target_pairs={{1,0},{2,1},{3,2},{5,4},{6,5},{7,6},{9,8},{10,9},{11,10},{13,12},{... | collective-permute-start | bytes 589832 | tf_op jit(solution)/shard_map/ppermute | solution.py:25
  88.5 8.5 %collective-permute-start.13 = (f32[2,192,128]{2,1,0:T(8,128)}, f32[2,192,128]{2,1,0:T(8,128)}, u32[]{:S(2)}, u32[]{:S(2)}) collective-permute-start(f32[2,192,128]{2,1,0:T(8,128)} %get-tuple-element.29), channel_id=1, source_target_pairs={{0,1},{1,2},{2,3},{4,5},{5,6},{6,7},{8,9},{9,10},{10,11},{12,13},{... | collective-permute-start | bytes 589832 | tf_op jit(solution)/shard_map/ppermute | solution.py:22
  98.9 1.8 %collective-permute-start.14 = (f32[4,192,128]{2,1,0:T(8,128)S(1)}, f32[4,192,128]{2,1,0:T(8,128)S(1)}, u32[]{:S(2)}, u32[]{:S(2)}) collective-permute-start(f32[4,192,128]{2,1,0:T(8,128)S(1)} %fusion.4), channel_id=1, source_target_pairs={{0,4},{4,0},{8,12},{12,8},{1,5},{5,1},{9,13},{13,9},{2,6},{6,2},{1... | collective-permute-start | bytes 1179656 | tf_op jit(solution)/shard_map/ppermute | solution.py:117
  100.7 11.2 %collective-permute-start.15 = (f32[4,192,128]{2,1,0:T(8,128)S(1)}, f32[4,192,128]{2,1,0:T(8,128)S(1)}, u32[]{:S(2)}, u32[]{:S(2)}) collective-permute-start(f32[4,192,128]{2,1,0:T(8,128)S(1)} %add.519), channel_id=1, source_target_pairs={{0,8},{4,12},{8,0},{12,4},{1,9},{5,13},{9,1},{13,5},{2,10},{6,14},... | collective-permute-start | bytes 1179656 | tf_op jit(solution)/shard_map/ppermute | solution.py:117
